TPU v7x, 128 devices: a whole 4x4x4 slice. The times are simulated.
128 devices in a mesh: wave: 32 (over x, y, core), lev: 4 (over z).
Axes of the slice: x: 4, y: 4, z: 4, core: 2. Of those that a mesh axis runs over, the one named last changes fastest.
Arguments:
- coefficients: bfloat16 [640, 640, 512], P('wave', 'lev'), may hold values from -6 to 6
- factors: bfloat16 [5, 2, 640, 20, 640], P(None, None, 'wave', None, 'lev'), may hold values from -1 to 1
- wave_ids: int32 [640], replicated, may hold values from 0 to 639, each once
Outputs:
- grid: bfloat16 [640, 256, 2560], P(('wave', 'lev'))
Inputs may be any that keep to these rules, and one draw needn't show every extreme that they name: `wave_ids`: each wavenumber 0 .. 639 appears exactly once.
All inputs are finite; a program needn't handle non-finite values.
Results may differ from a plain program's by a relative error of at most 0.0079.
Values may be sent and summed in bfloat16 or wider, within the bound.
No kernel may reach another device: no remote copies, remote signals or barrier semaphores. Data moves between devices by JAX's collectives and lax.ppermute only.
A program may use at most 64 MiB of HBM per device.

v0:
```python
import math
import jax
import jax.numpy as jnp
from jax import lax
from jax.sharding import PartitionSpec as P

NLON = 2560


def swapped(block, axis, apart):
    count = lax.axis_size(axis)
    route = []
    for low in range(count):
        high = low | 1 << apart
        if high != low and high < count:
            route += [(low, high), (high, low)]
    return lax.ppermute(block, axis, route)


def body(coefficients, factors, wave_ids):
    wave_count = lax.axis_size("wave")
    sections = wave_count.bit_length() - 1
    deg_block = coefficients.shape[0]
    wave_block = coefficients.shape[1]
    channels = coefficients.shape[2]
    total_waves = wave_ids.shape[0]
    wave_pos = lax.axis_index("wave")
    lev_pos = lax.axis_index("lev")
    own_ids = lax.dynamic_slice_in_dim(wave_ids, lev_pos * wave_block, wave_block, 0)
    degree = wave_pos * deg_block + jnp.arange(deg_block, dtype=jnp.int32)
    live_mask = (degree[:, None] >= own_ids[None, :])[:, :, None]
    current = jnp.where(live_mask, coefficients, jnp.zeros((), coefficients.dtype))
    for section in range(sections):
        partner = swapped(current, "wave", section)
        combined = jnp.einsum(
            "oim,imc->omc", factors[section, 0], current, preferred_element_type=jnp.float32
        )
        combined = combined + jnp.einsum(
            "oim,imc->omc", factors[section, 1], partner, preferred_element_type=jnp.float32
        )
        current = combined.astype(jnp.bfloat16)
    grid_rows = lax.all_to_all(current, "lev", split_axis=0, concat_axis=1, tiled=True)
    longitude = jnp.arange(NLON, dtype=jnp.int32)
    phases = wave_ids[:, None] * longitude[None, :] % NLON
    angles = phases.astype(jnp.float32) * (2.0 * math.pi / NLON)
    weight = jnp.where(wave_ids == 0, 1.0, 2.0).astype(jnp.float32) / math.sqrt(2.0 * total_waves)
    cosine_part = weight[:, None] * jnp.cos(angles)
    sine_part = -weight[:, None] * jnp.sin(angles)
    fourier_table = jnp.stack([cosine_part, sine_part], axis=1).astype(jnp.bfloat16)
    lat_count = grid_rows.shape[0]
    split_rows = grid_rows.reshape(lat_count, total_waves, 2, channels // 2)
    synthesized = jnp.einsum(
        "rmpc,mpj->rcj", split_rows, fourier_table, preferred_element_type=jnp.float32
    )
    return synthesized.astype(jnp.bfloat16)


def solution(mesh):
    in_specs = (P("wave", "lev", None), P(None, None, "wave", None, "lev"), P())
    out_specs = P(("wave", "lev"), None, None)
    return jax.shard_map(body, mesh=mesh, in_specs=in_specs, out_specs=out_specs, check_vma=False)
```

profile of v0, /device:TPU:0, one launch (start us, length us, event | category | flops | bytes accessed | tf_op | source)
XLA Modules:
  0.0 417.2 jit_solution(2084151253647331986)
XLA Ops:
  3.3 4.6 %fusion.50 = (bf16[1,1,20,20,160]{4,1,3,2,0:T(2,128)(2,1)}, bf16[1,1,20,20,160]{4,1,3,2,0:T(2,128)(2,1)}, bf16[1,1,20,20,160]{4,1,3,2,0:T(2,128)(2,1)}, bf16[1,1...) fusion(bf16[5,2,20,20,160]{4,1,3,2,0:T(2,128)(2,1)S(1)} %copy-d, ...), kind=kLoop, calls=%fused_computation.55 | loop fusion | bytes 2560000 | tf_op jit(solution)/shard_map/slice | solution.py:39
  11.0 3.1 copy.57
  14.1 3.4 fusion.22
  17.5 5.0 %fusion.7 = bf16[20,160,512]{2,0,1:T(8,128)(2,1)S(1)} fusion(f32[160,512,20]{1,2,0:T(8,128)S(1)} %fusion.22, bf16[20,160,512]{2,1,0:T(8,128)(2,1)} %collective-permute-done, bf16[1,1,20,20,160]{3,2,4,1,0:T(8,128)(2,1)S(1)} %copy-done.9), kind=kOutput, calls=%fused_computation.18 | convolution fusion | flops 68812800 | bytes 13235200 | tf_op jit(solution)/shard_map/oim,imc->omc/dot_general | solution.py:38
  29.0 3.1 copy.58
  32.1 3.1 copy.59
  35.2 3.6 fusion.44
  38.9 61.9 %collective-permute-done.1 = bf16[20,160,512]{2,1,0:T(8,128)(2,1)S(1)} collective-permute-done((bf16[20,160,512]{2,1,0:T(8,128)(2,1)}, bf16[20,160,512]{2,1,0:T(8,128)(2,1)S(1)}, u32[]{:S(2)}, u32[]{:S(2)}) %collective-permute-start.1) | collective-permute-done | bytes 3276832 | tf_op jit(solution)/shard_map/ppermute | solution.py:17
  108.6 3.3 collective-permute-start.2
  115.0 3.1 copy.61
  118.1 3.6 fusion.41
  121.8 61.1 %collective-permute-done.2 = bf16[20,160,512]{2,1,0:T(8,128)(2,1)S(1)} collective-permute-done((bf16[20,160,512]{2,1,0:T(8,128)(2,1)}, bf16[20,160,512]{2,1,0:T(8,128)(2,1)S(1)}, u32[]{:S(2)}, u32[]{:S(2)}) %collective-permute-start.2) | collective-permute-done | bytes 3276832 | tf_op jit(solution)/shard_map/ppermute | solution.py:17
  195.3 3.1 copy.63
  198.5 3.6 fusion.38
  202.1 60.4 %collective-permute-done.3 = bf16[20,160,512]{2,1,0:T(8,128)(2,1)S(1)} collective-permute-done((bf16[20,160,512]{2,1,0:T(8,128)(2,1)}, bf16[20,160,512]{2,1,0:T(8,128)(2,1)S(1)}, u32[]{:S(2)}, u32[]{:S(2)}) %collective-permute-start.3) | collective-permute-done | bytes 3276832 | tf_op jit(solution)/shard_map/ppermute | solution.py:17
  276.5 3.1 copy.65
  279.6 3.6 fusion.35
  283.2 59.5 %collective-permute-done.4 = bf16[20,160,512]{2,1,0:T(8,128)(2,1)S(1)} collective-permute-done((bf16[20,160,512]{2,1,0:T(8,128)(2,1)}, bf16[20,160,512]{2,1,0:T(8,128)(2,1)S(1)}, u32[]{:S(2)}, u32[]{:S(2)}) %collective-permute-start.4) | collective-permute-done | bytes 3276832 | tf_op jit(solution)/shard_map/ppermute | solution.py:17
  348.7 5.4 %all-to-all-start = ((bf16[20,160,512]{2,1,0:T(8,128)(2,1)}), bf16[20,160,512]{2,1,0:T(8,128)(2,1)S(1)}, u32[]{:S(2)}, u32[]{:S(2)}) async-start(bf16[20,160,512]{2,1,0:T(8,128)(2,1)} %copy.50), calls=%async_computation | async-start | bytes 6553600 | tf_op jit(solution)/shard_map/all_to_all | solution.py:42
  354.1 29.7 %multiply_convert_fusion.1 = (bf16[640,1,2560]{2,0,1:T(8,128)(2,1)}, bf16[640,1,2560]{2,0,1:T(8,128)(2,1)}) fusion(s32[640]{0:T(1024)S(1)} %copy-done.11, f32[640]{0:T(1024)S(1)} %get-tuple-element.17, f32[640]{0:T(1024)S(1)} %get-tuple-element.18), kind=kLoop, calls=%fused_computation.13 | loop fusion | flops 21299200 | bytes 6561280 | tf_op jit(solution)/shard_map/convert
  383.9 6.4 %all-to-all-done = bf16[20,160,512]{2,1,0:T(8,128)(2,1)S(1)} async-done(((bf16[20,160,512]{2,1,0:T(8,128)(2,1)}), bf16[20,160,512]{2,1,0:T(8,128)(2,1)S(1)}, u32[]{:S(2)}, u32[]{:S(2)}) %all-to-all-start) | async-done | bytes 3276832 | tf_op jit(solution)/shard_map/all_to_all | solution.py:42
  390.2 5.7 %copy.54 = bf16[5,4,160,512]{2,1,3,0:T(4,128)(2,1)} copy(bf16[5,4,160,512]{3,2,0,1:T(8,128)(2,1)S(1)} %bitcast.56) | data formatting | bytes 6553600 | tf_op jit(solution)/shard_map/reshape | solution.py:51
  395.9 8.3 %reshape.156 = bf16[5,640,2,256]{1,3,2,0:T(8,128)(2,1)} reshape(bf16[5,4,160,512]{2,1,3,0:T(4,128)(2,1)} %copy.54) | data formatting | bytes 6553600 | tf_op jit(solution)/shard_map/reshape | solution.py:51
  404.3 12.9 %bitcast_convert_fusion = bf16[5,256,2560]{2,1,0:T(8,128)(2,1)} fusion(bf16[5,640,2,256]{1,3,2,0:T(8,128)(2,1)} %reshape.156, bf16[640,1,2560]{2,0,1:T(8,128)(2,1)} %get-tuple-element.16, bf16[640,1,2560]{2,0,1:T(8,128)(2,1)S(1)} %copy-done.10), kind=kOutput, calls=%fused_computation | convolution fusion | flops 8395161600 | bytes 16384000 | tf_op jit(solution)/shard_map/rmpc,mpj->rcj/dot_general | solution.py:52
  (47 shorter events, 56.0 us)
Async XLA Ops:
  0.0 3.3 copy-start.4
  3.2 14.3 %collective-permute-start = (bf16[20,160,512]{2,1,0:T(8,128)(2,1)S(1)}, bf16[20,160,512]{2,1,0:T(8,128)(2,1)}, u32[]{:S(2)}, u32[]{:S(2)}) collective-permute-start(bf16[20,160,512]{2,1,0:T(8,128)(2,1)S(1)} %broadcast_select_fusion), channel_id=1, source_target_pairs={{0,4},{4,0},{8,12},{12,8},{16,20},{20,16},{24,28},{28,24},{32,36},... | collective-permute-start | bytes 9830408 | tf_op jit(solution)/shard_map/ppermute | solution.py:17
  14.1 3.4 copy-start.9
  22.6 1.9 copy-start.1
  27.3 73.5 %collective-permute-start.1 = (bf16[20,160,512]{2,1,0:T(8,128)(2,1)}, bf16[20,160,512]{2,1,0:T(8,128)(2,1)S(1)}, u32[]{:S(2)}, u32[]{:S(2)}) collective-permute-start(bf16[20,160,512]{2,1,0:T(8,128)(2,1)} %copy.35), channel_id=1, source_target_pairs={{0,8},{8,0},{4,12},{12,4},{16,24},{24,16},{20,28},{28,20},{32,40},... | collective-permute-start | bytes 9830408 | tf_op jit(solution)/shard_map/ppermute | solution.py:17
  35.2 65.6 %copy-start.5 = (bf16[1,1,20,20,160]{3,2,4,1,0:T(8,128)(2,1)S(1)}, bf16[1,1,20,20,160]{3,2,4,1,0:T(8,128)(2,1)}, u32[]{:S(2)}) copy-start(bf16[1,1,20,20,160]{3,2,4,1,0:T(8,128)(2,1)} %copy.59) | copy-start | bytes 384004
  103.9 1.9 copy-start.2
  108.6 74.3 %collective-permute-start.2 = (bf16[20,160,512]{2,1,0:T(8,128)(2,1)}, bf16[20,160,512]{2,1,0:T(8,128)(2,1)S(1)}, u32[]{:S(2)}, u32[]{:S(2)}) collective-permute-start(bf16[20,160,512]{2,1,0:T(8,128)(2,1)} %copy.39), channel_id=1, source_target_pairs={{0,16},{16,0},{4,20},{20,4},{8,24},{24,8},{12,28},{28,12},{32,48},... | collective-permute-start | bytes 9830408 | tf_op jit(solution)/shard_map/ppermute | solution.py:17
  118.1 64.7 %copy-start.6 = (bf16[1,1,20,20,160]{3,2,4,1,0:T(8,128)(2,1)S(1)}, bf16[1,1,20,20,160]{3,2,4,1,0:T(8,128)(2,1)}, u32[]{:S(2)}) copy-start(bf16[1,1,20,20,160]{3,2,4,1,0:T(8,128)(2,1)} %copy.61) | copy-start | bytes 384004
  185.9 1.9 copy-start.3
  190.7 71.9 %collective-permute-start.3 = (bf16[20,160,512]{2,1,0:T(8,128)(2,1)}, bf16[20,160,512]{2,1,0:T(8,128)(2,1)S(1)}, u32[]{:S(2)}, u32[]{:S(2)}) collective-permute-start(bf16[20,160,512]{2,1,0:T(8,128)(2,1)} %copy.43), channel_id=1, source_target_pairs={{0,32},{32,0},{4,36},{36,4},{8,40},{40,8},{12,44},{44,12},{16,48},... | collective-permute-start | bytes 9830408 | tf_op jit(solution)/shard_map/ppermute | solution.py:17
  198.5 64.1 %copy-start.7 = (bf16[1,1,20,20,160]{3,2,4,1,0:T(8,128)(2,1)S(1)}, bf16[1,1,20,20,160]{3,2,4,1,0:T(8,128)(2,1)}, u32[]{:S(2)}) copy-start(bf16[1,1,20,20,160]{3,2,4,1,0:T(8,128)(2,1)} %copy.63) | copy-start | bytes 384004
  265.6 1.9 copy-start
  270.3 72.5 %collective-permute-start.4 = (bf16[20,160,512]{2,1,0:T(8,128)(2,1)}, bf16[20,160,512]{2,1,0:T(8,128)(2,1)S(1)}, u32[]{:S(2)}, u32[]{:S(2)}) collective-permute-start(bf16[20,160,512]{2,1,0:T(8,128)(2,1)} %copy.47), channel_id=1, source_target_pairs={{0,64},{64,0},{4,68},{68,4},{8,72},{72,8},{12,76},{76,12},{16,80},... | collective-permute-start | bytes 9830408 | tf_op jit(solution)/shard_map/ppermute | solution.py:17
  279.6 63.2 %copy-start.8 = (bf16[1,1,20,20,160]{3,2,4,1,0:T(8,128)(2,1)S(1)}, bf16[1,1,20,20,160]{3,2,4,1,0:T(8,128)(2,1)}, u32[]{:S(2)}) copy-start(bf16[1,1,20,20,160]{3,2,4,1,0:T(8,128)(2,1)} %copy.65) | copy-start | bytes 384004
  348.7 5.4 %copy-start.11 = (s32[640]{0:T(1024)S(1)}, s32[640]{0:T(1024)}, u32[]{:S(2)}) copy-start(s32[640]{0:T(1024)} %param.5) | copy-start | bytes 7684
  348.7 41.6 %all-to-all-start = ((bf16[20,160,512]{2,1,0:T(8,128)(2,1)}), bf16[20,160,512]{2,1,0:T(8,128)(2,1)S(1)}, u32[]{:S(2)}, u32[]{:S(2)}) async-start(bf16[20,160,512]{2,1,0:T(8,128)(2,1)} %copy.50), calls=%async_computation | async-start | bytes 6553600 | tf_op jit(solution)/shard_map/all_to_all | solution.py:42
  395.9 8.3 %copy-start.10 = (bf16[640,1,2560]{2,0,1:T(8,128)(2,1)S(1)}, bf16[640,1,2560]{2,0,1:T(8,128)(2,1)}, u32[]{:S(2)}) copy-start(bf16[640,1,2560]{2,0,1:T(8,128)(2,1)} %get-tuple-element.15) | copy-start | bytes 9830404
where the time goes:
time: 418 us; the launch traced here: 417 us
  waiting for transfers between devices  249 us (60%)
  local copies, waits for them, and re-layouts  72.5 us (17%)
  matrix products  48.1 us (12%)
  other arithmetic  32 us (8%)
  starting transfers between devices  15 us (4%)
    ppermute x5, waiting for transfers between devices, swapped(): return lax.ppermute(block, axis, route)  243 us
    unnamed x34, local copies, waits for them, and re-layouts  39 us
    another operation x1, other arithmetic  29.7 us
    dot_general x5, matrix products, body(): jnp.einsum('oim,imc->omc', factors[section, 0], current, preferred_elemen...  17.9 us
    dot_general x5, matrix products, body(): jnp.einsum('oim,imc->omc', factors[section, 1], partner, preferred_elemen...  17.3 us
    convert_element_type x5, local copies, waits for them, and re-layouts, body(): current = combined.astype(jnp.bfloat16)  14 us
    reshape x2, local copies, waits for them, and re-layouts, body(): split_rows = grid_rows.reshape(lat_count, total_waves, 2, channels // 2)  14 us
    dot_general x1, matrix products, body(): jnp.einsum('rmpc,mpj->rcj', split_rows, fourier_table, preferred_element_...  12.9 us
  transfers between devices with their start and end apart: 6, of which 5 were waited for; matrix products, arithmetic and copies ran while one was open for 20% of the time, Pallas kernels for 0%

commit v1 on v0

--- a/solution.py
+++ b/solution.py
@@ -5,6 +5,22 @@
 from jax.sharding import PartitionSpec as P
 
 NLON = 2560
+
+
+def swapped_with_each(shard, axis, split, join):
+    ways, here = (lax.axis_size(axis), lax.axis_index(axis))
+    width = shard.shape[split] // ways
+    shape = list(shard.shape)
+    shape[split] = width
+    height = shape[join]
+    shape[join] = height * ways
+    full = jnp.zeros(shape, shard.dtype)
+    for mask in range(ways):
+        part = lax.dynamic_slice_in_dim(shard, (here ^ mask) * width, width, axis=split)
+        if mask:
+            part = lax.ppermute(part, axis, [(d, d ^ mask) for d in range(ways)])
+        full = lax.dynamic_update_slice_in_dim(full, part, (here ^ mask) * height, axis=join)
+    return full
 
 
 def swapped(block, axis, apart):
@@ -39,7 +55,7 @@
             "oim,imc->omc", factors[section, 1], partner, preferred_element_type=jnp.float32
         )
         current = combined.astype(jnp.bfloat16)
-    grid_rows = lax.all_to_all(current, "lev", split_axis=0, concat_axis=1, tiled=True)
+    grid_rows = swapped_with_each(current, "lev", 0, 1)
     longitude = jnp.arange(NLON, dtype=jnp.int32)
     phases = wave_ids[:, None] * longitude[None, :] % NLON
     angles = phases.astype(jnp.float32) * (2.0 * math.pi / NLON)

time: 418 us -> 470 us (1.12); the launches traced: 417 us -> 462 us
  local copies, waits for them, and re-layouts: 72.5 us -> 122 us
  waiting for transfers between devices: 249 us -> 243 us
    dynamic_update_slice x0 -> x4, local copies, waits for them, and re-layouts: none -> 53.8 us  [swapped_with_each(): lax.dynamic_update_slice_in_dim(full, part, (here ^ mask) * height, axis=...]
    reshape x2 -> x0, local copies, waits for them, and re-layouts: 14 us -> none  [body(): split_rows = grid_rows.reshape(lat_count, total_waves, 2, channels // 2)]
    all_to_all x1 -> x0, waiting for transfers between devices: 6.38 us -> none  [body(): lax.all_to_all(current, 'lev', split_axis=0, concat_axis=1, tiled=True)]
    ppermute x0 -> x3, starting transfers between devices: none -> 5.78 us  [swapped_with_each(): part = lax.ppermute(part, axis, [(d, d ^ mask) for d in range(ways)])]
    dynamic_slice x0 -> x5, local copies, waits for them, and re-layouts: none -> 5.61 us  [swapped_with_each(): lax.dynamic_slice_in_dim(shard, (here ^ mask) * width, width, axis=split)]
    all_to_all x1 -> x0, starting transfers between devices: 5.44 us -> none  [body(): lax.all_to_all(current, 'lev', split_axis=0, concat_axis=1, tiled=True)]
    convert_element_type x5 -> x4, local copies, waits for them, and re-layouts: 14 us -> 11.2 us  [body(): current = combined.astype(jnp.bfloat16)]
    unnamed x34 -> x32, local copies, waits for them, and re-layouts: 39 us -> 39.1 us
  transfers between devices with their start and end apart: 6 -> 8, of which waited for: 5 -> 4; matrix products, arithmetic and copies ran while one was open for 20% -> 28% of each run, Pallas kernels for 0% -> 0%
where the time goes in v1:
time: 470 us; the launch traced here: 462 us
  waiting for transfers between devices  243 us (52%)
  local copies, waits for them, and re-layouts  122 us (26%)
  matrix products  48.7 us (10%)
  other arithmetic  32 us (7%)
  starting transfers between devices  16 us (3%)
    ppermute x5, waiting for transfers between devices, swapped(): return lax.ppermute(block, axis, route)  243 us
    dynamic_update_slice x4, local copies, waits for them, and re-layouts, swapped_with_each(): lax.dynamic_update_slice_in_dim(full, part, (here ^ mask) * height, axis=...  53.8 us
    unnamed x32, local copies, waits for them, and re-layouts  39.1 us
    another operation x1, other arithmetic  29.7 us
    dot_general x5, matrix products, body(): jnp.einsum('oim,imc->omc', factors[section, 0], current, preferred_elemen...  17.9 us
    dot_general x5, matrix products, body(): jnp.einsum('oim,imc->omc', factors[section, 1], partner, preferred_elemen...  17.3 us
    dot_general x1, matrix products, body(): jnp.einsum('rmpc,mpj->rcj', split_rows, fourier_table, preferred_element_...  13.5 us
    convert_element_type x4, local copies, waits for them, and re-layouts, body(): current = combined.astype(jnp.bfloat16)  11.2 us
  transfers between devices with their start and end apart: 8, of which 4 were waited for; matrix products, arithmetic and copies ran while one was open for 28% of the time, Pallas kernels for 0%

profile of v1, /device:TPU:0, one launch (start us, length us, event | category | flops | bytes accessed | tf_op | source)
XLA Modules:
  0.0 461.6 jit_solution(3450515387603865606)
XLA Ops:
  3.3 4.6 fusion.49
  11.0 3.1 copy.46
  14.2 3.4 fusion.21
  17.6 5.0 %fusion.7 = bf16[20,160,512]{2,0,1:T(8,128)(2,1)S(1)} fusion(f32[160,512,20]{1,2,0:T(8,128)S(1)} %fusion.21, bf16[20,160,512]{2,1,0:T(8,128)(2,1)} %collective-permute-done, bf16[1,1,20,20,160]{3,2,4,1,0:T(8,128)(2,1)S(1)} %copy-done.9), kind=kOutput, calls=%fused_computation.18 | convolution fusion | flops 68812800 | bytes 13235200 | tf_op jit(solution)/shard_map/oim,imc->omc/dot_general | solution.py:54
  29.4 3.1 copy.47
  35.7 3.6 fusion.43
  39.3 61.9 %collective-permute-done.1 = bf16[20,160,512]{2,1,0:T(8,128)(2,1)S(1)} collective-permute-done((bf16[20,160,512]{2,1,0:T(8,128)(2,1)}, bf16[20,160,512]{2,1,0:T(8,128)(2,1)S(1)}, u32[]{:S(2)}, u32[]{:S(2)}) %collective-permute-start.1) | collective-permute-done | bytes 3276832 | tf_op jit(solution)/shard_map/ppermute | solution.py:33
  109.1 3.3 collective-permute-start.2
  112.3 3.1 copy.49
  118.6 3.6 fusion.40
  122.3 61.1 %collective-permute-done.2 = bf16[20,160,512]{2,1,0:T(8,128)(2,1)S(1)} collective-permute-done((bf16[20,160,512]{2,1,0:T(8,128)(2,1)}, bf16[20,160,512]{2,1,0:T(8,128)(2,1)S(1)}, u32[]{:S(2)}, u32[]{:S(2)}) %collective-permute-start.2) | collective-permute-done | bytes 3276832 | tf_op jit(solution)/shard_map/ppermute | solution.py:33
  192.8 3.1 copy.51
  199.1 3.6 fusion.37
  202.7 60.4 %collective-permute-done.3 = bf16[20,160,512]{2,1,0:T(8,128)(2,1)S(1)} collective-permute-done((bf16[20,160,512]{2,1,0:T(8,128)(2,1)}, bf16[20,160,512]{2,1,0:T(8,128)(2,1)S(1)}, u32[]{:S(2)}, u32[]{:S(2)}) %collective-permute-start.3) | collective-permute-done | bytes 3276832 | tf_op jit(solution)/shard_map/ppermute | solution.py:33
  274.0 3.1 copy.53
  280.3 3.6 fusion.34
  283.9 59.5 %collective-permute-done.4 = bf16[20,160,512]{2,1,0:T(8,128)(2,1)S(1)} collective-permute-done((bf16[20,160,512]{2,1,0:T(8,128)(2,1)}, bf16[20,160,512]{2,1,0:T(8,128)(2,1)S(1)}, u32[]{:S(2)}, u32[]{:S(2)}) %collective-permute-start.4) | collective-permute-done | bytes 3276832 | tf_op jit(solution)/shard_map/ppermute | solution.py:33
  352.8 3.8 collective-permute-start.6
  357.0 29.7 %multiply_convert_fusion.1 = (bf16[640,1,2560]{2,0,1:T(8,128)(2,1)}, bf16[640,1,2560]{2,0,1:T(8,128)(2,1)}) fusion(s32[640]{0:T(1024)S(1)} %copy-done.10, f32[640]{0:T(1024)S(1)} %get-tuple-element.21, f32[640]{0:T(1024)S(1)} %get-tuple-element.22), kind=kLoop, calls=%fused_computation.13 | loop fusion | flops 21299200 | bytes 6561280 | tf_op jit(solution)/shard_map/convert
  389.6 12.5 %dynamic_update_slice.12 = bf16[5,640,512]{1,2,0:T(8,128)(2,1)} dynamic-update-slice(bf16[5,640,512]{1,2,0:T(8,128)(2,1)} %broadcast_in_dim.30, bf16[5,160,512]{1,2,0:T(8,128)(2,1)S(1)} %copy.37, s32[]{:T(128)} %constant.11.clone.1, s32[]{:T(128)S(6)} %select_n.51, s32[]{:T(128)} %constant.11.clone.1) | dynamic-update-slice | bytes 1638404 | tf_op jit(solution)/shard_map/dynamic_update_slice | solution.py:22
  403.6 14.1 %dynamic_update_slice.13 = bf16[5,640,512]{1,2,0:T(8,128)(2,1)} dynamic-update-slice(bf16[5,640,512]{1,2,0:T(8,128)(2,1)} %dynamic_update_slice.12, bf16[5,160,512]{1,2,0:T(8,128)(2,1)S(1)} %copy.39, s32[]{:T(128)} %constant.11.clone.1, s32[]{:T(128)S(6)} %select_n.55, s32[]{:T(128)} %constant.11.clone.1) | dynamic-update-slice | bytes 1638404 | tf_op jit(solution)/shard_map/dynamic_update_slice | solution.py:22
  419.2 13.9 %dynamic_update_slice.14 = bf16[5,640,512]{1,2,0:T(8,128)(2,1)} dynamic-update-slice(bf16[5,640,512]{1,2,0:T(8,128)(2,1)} %dynamic_update_slice.13, bf16[5,160,512]{1,2,0:T(8,128)(2,1)S(1)} %copy.41, s32[]{:T(128)} %constant.11.clone.1, s32[]{:T(128)S(6)} %select_n.57, s32[]{:T(128)} %constant.11.clone.1) | dynamic-update-slice | bytes 1638404 | tf_op jit(solution)/shard_map/dynamic_update_slice | solution.py:22
  434.6 13.3 %dynamic_update_slice.15 = bf16[5,640,512]{1,2,0:T(8,128)(2,1)} dynamic-update-slice(bf16[5,640,512]{1,2,0:T(8,128)(2,1)} %dynamic_update_slice.14, bf16[5,160,512]{1,2,0:T(8,128)(2,1)S(1)} %copy.43, s32[]{:T(128)} %constant.11.clone.1, s32[]{:T(128)S(6)} %select_n.59, s32[]{:T(128)} %constant.11.clone.1) | dynamic-update-slice | bytes 1638404 | tf_op jit(solution)/shard_map/dynamic_update_slice | solution.py:22
  447.9 13.5 %bitcast_convert_fusion = bf16[5,256,2560]{2,1,0:T(8,128)(2,1)} fusion(bf16[5,640,2,256]{1,3,2,0:T(8,128)(2,1)} %bitcast.58, bf16[640,1,2560]{2,0,1:T(8,128)(2,1)} %get-tuple-element.20, bf16[640,1,2560]{2,0,1:T(8,128)(2,1)} %get-tuple-element.19), kind=kOutput, calls=%fused_computation | convolution fusion | flops 8395161600 | bytes 16384000 | tf_op jit(solution)/shard_map/rmpc,mpj->rcj/dot_general | solution.py:68
  (59 shorter events, 71.0 us)
Async XLA Ops:
  0.0 3.3 copy-start.4
  3.2 14.3 %collective-permute-start = (bf16[20,160,512]{2,1,0:T(8,128)(2,1)S(1)}, bf16[20,160,512]{2,1,0:T(8,128)(2,1)}, u32[]{:S(2)}, u32[]{:S(2)}) collective-permute-start(bf16[20,160,512]{2,1,0:T(8,128)(2,1)S(1)} %broadcast_select_fusion), channel_id=1, source_target_pairs={{0,4},{4,0},{8,12},{12,8},{16,20},{20,16},{24,28},{28,24},{32,36},... | collective-permute-start | bytes 9830408 | tf_op jit(solution)/shard_map/ppermute | solution.py:33
  14.2 3.4 copy-start.9
  22.6 1.9 copy-start.1
  27.3 74.0 %collective-permute-start.1 = (bf16[20,160,512]{2,1,0:T(8,128)(2,1)}, bf16[20,160,512]{2,1,0:T(8,128)(2,1)S(1)}, u32[]{:S(2)}, u32[]{:S(2)}) collective-permute-start(bf16[20,160,512]{2,1,0:T(8,128)(2,1)} %copy.22), channel_id=1, source_target_pairs={{0,8},{8,0},{4,12},{12,4},{16,24},{24,16},{20,28},{28,20},{32,40},... | collective-permute-start | bytes 9830408 | tf_op jit(solution)/shard_map/ppermute | solution.py:33
  35.7 65.6 %copy-start.6 = (bf16[1,1,20,20,160]{3,2,4,1,0:T(8,128)(2,1)S(1)}, bf16[1,1,20,20,160]{3,2,4,1,0:T(8,128)(2,1)}, u32[]{:S(2)}) copy-start(bf16[1,1,20,20,160]{3,2,4,1,0:T(8,128)(2,1)} %copy.48) | copy-start | bytes 384004
  104.3 1.9 copy-start.2
  109.1 74.3 %collective-permute-start.2 = (bf16[20,160,512]{2,1,0:T(8,128)(2,1)}, bf16[20,160,512]{2,1,0:T(8,128)(2,1)S(1)}, u32[]{:S(2)}, u32[]{:S(2)}) collective-permute-start(bf16[20,160,512]{2,1,0:T(8,128)(2,1)} %copy.26), channel_id=1, source_target_pairs={{0,16},{16,0},{4,20},{20,4},{8,24},{24,8},{12,28},{28,12},{32,48},... | collective-permute-start | bytes 9830408 | tf_op jit(solution)/shard_map/ppermute | solution.py:33
  118.6 64.7 %copy-start.7 = (bf16[1,1,20,20,160]{3,2,4,1,0:T(8,128)(2,1)S(1)}, bf16[1,1,20,20,160]{3,2,4,1,0:T(8,128)(2,1)}, u32[]{:S(2)}) copy-start(bf16[1,1,20,20,160]{3,2,4,1,0:T(8,128)(2,1)} %copy.50) | copy-start | bytes 384004
  186.4 1.9 copy-start.3
  191.1 72.0 %collective-permute-start.3 = (bf16[20,160,512]{2,1,0:T(8,128)(2,1)}, bf16[20,160,512]{2,1,0:T(8,128)(2,1)S(1)}, u32[]{:S(2)}, u32[]{:S(2)}) collective-permute-start(bf16[20,160,512]{2,1,0:T(8,128)(2,1)} %copy.30), channel_id=1, source_target_pairs={{0,32},{32,0},{4,36},{36,4},{8,40},{40,8},{12,44},{44,12},{16,48},... | collective-permute-start | bytes 9830408 | tf_op jit(solution)/shard_map/ppermute | solution.py:33
  199.1 64.1 %copy-start.8 = (bf16[1,1,20,20,160]{3,2,4,1,0:T(8,128)(2,1)S(1)}, bf16[1,1,20,20,160]{3,2,4,1,0:T(8,128)(2,1)}, u32[]{:S(2)}) copy-start(bf16[1,1,20,20,160]{3,2,4,1,0:T(8,128)(2,1)} %copy.52) | copy-start | bytes 384004
  266.2 1.9 copy-start
  268.1 12.1 %copy-start.10 = (s32[640]{0:T(1024)S(1)}, s32[640]{0:T(1024)}, u32[]{:S(2)}) copy-start(s32[640]{0:T(1024)} %param.5) | copy-start | bytes 7684
  270.9 72.4 %collective-permute-start.4 = (bf16[20,160,512]{2,1,0:T(8,128)(2,1)}, bf16[20,160,512]{2,1,0:T(8,128)(2,1)S(1)}, u32[]{:S(2)}, u32[]{:S(2)}) collective-permute-start(bf16[20,160,512]{2,1,0:T(8,128)(2,1)} %copy.34), channel_id=1, source_target_pairs={{0,64},{64,0},{4,68},{68,4},{8,72},{72,8},{12,76},{76,12},{16,80},... | collective-permute-start | bytes 9830408 | tf_op jit(solution)/shard_map/ppermute | solution.py:33
  280.3 63.1 %copy-start.5 = (bf16[1,1,20,20,160]{3,2,4,1,0:T(8,128)(2,1)S(1)}, bf16[1,1,20,20,160]{3,2,4,1,0:T(8,128)(2,1)}, u32[]{:S(2)}) copy-start(bf16[1,1,20,20,160]{3,2,4,1,0:T(8,128)(2,1)} %copy.54) | copy-start | bytes 384004
  349.7 52.3 %collective-permute-start.5 = (bf16[5,160,512]{2,1,0:T(8,128)(2,1)}, bf16[5,160,512]{2,1,0:T(8,128)(2,1)}, u32[]{:S(2)}, u32[]{:S(2)}) collective-permute-start(bf16[5,160,512]{2,1,0:T(8,128)(2,1)} %copy.38), channel_id=1, source_target_pairs={{0,1},{1,0},{2,3},{3,2},{4,5},{5,4},{6,7},{7,6},{8,9},{9,8},{10,11... | collective-permute-start | bytes 2457608 | tf_op jit(solution)/shard_map/ppermute | solution.py:21
  352.8 64.9 %collective-permute-start.6 = (bf16[5,160,512]{2,1,0:T(8,128)(2,1)}, bf16[5,160,512]{2,1,0:T(8,128)(2,1)}, u32[]{:S(2)}, u32[]{:S(2)}) collective-permute-start(bf16[5,160,512]{2,1,0:T(8,128)(2,1)} %copy.40), channel_id=1, source_target_pairs={{0,2},{1,3},{2,0},{3,1},{4,6},{5,7},{6,4},{7,5},{8,10},{9,11},{10,... | collective-permute-start | bytes 2457608 | tf_op jit(solution)/shard_map/ppermute | solution.py:21
  356.9 76.2 %collective-permute-start.7 = (bf16[5,160,512]{2,1,0:T(8,128)(2,1)S(1)}, bf16[5,160,512]{2,1,0:T(8,128)(2,1)}, u32[]{:S(2)}, u32[]{:S(2)}) collective-permute-start(bf16[5,160,512]{2,1,0:T(8,128)(2,1)S(1)} %copy.42), channel_id=1, source_target_pairs={{0,3},{1,2},{2,1},{3,0},{4,7},{5,6},{6,5},{7,4},{8,11},{9,10},{10,... | collective-permute-start | bytes 2457608 | tf_op jit(solution)/shard_map/ppermute | solution.py:21
